TPU v7x, 256 devices: a whole 4x4x8 slice. The times are simulated.
256 devices in a mesh: req: 32 (over z_hi, y, core), tp: 8 (over x, z_lo).
Axes of the slice: x: 4, y: 4, z: 8 (z_hi: 4, z_lo: 2; z = z_hi * 2 + z_lo), core: 2. Of those that a mesh axis runs over, the one named last changes fastest.
Arguments:
- suffix: bfloat16 [256, 64, 2048], P('tp', 'req')
- prefix_store: bfloat16 [32, 2048, 2, 2048], P('req', None, None, 'tp')
- prefix_owner: int32 [2], replicated, may hold values from 0 to 31, as said below
- prefix_group: int32 [64], replicated, may hold values from 0 to 1
- request_perm: int32 [64], replicated, may hold values from 0 to 63, each once
- suffix_len: int32 [64], replicated, may hold values from 1 to 256, 8192 in all
- ln_gain_attn: float32 [2048], replicated, may hold values from 0.1 to 1.9
- w_qkv: bfloat16 [2048, 3, 2048], P(None, None, 'tp'), may hold values from -0.125 to 0.125
- w_out_attn: bfloat16 [2048, 2048], P('tp'), may hold values from -2.390625 to 2.390625
- ln_gain_mlp: float32 [2048], replicated, may hold values from 0.1 to 1.9
- w_in: bfloat16 [2048, 5120], P(None, 'tp'), may hold values from -0.125 to 0.125
- w_down: bfloat16 [5120, 2048], P('tp'), may hold values from -0.078125 to 0.078125
Outputs:
- layer_out: bfloat16 [256, 64, 2048], P('tp', 'req')
Inputs may be any that keep to these rules, and one draw needn't show every extreme that they name: `prefix_owner`: 2 different block indices. `request_perm`: each request exactly once.
All inputs are finite; a program needn't handle non-finite values.
Results may differ from a plain program's by a relative error of at most 0.015.
The roundings to bfloat16 on the way count: a program that leaves them out, or rounds other values in their place, can miss the bound.
Values may be sent and summed in bfloat16 or wider, within the bound.
A program may use at most 64 MiB of HBM per device.

v0:
```python
import jax
import jax.numpy as jnp
from jax import lax
from jax.sharding import PartitionSpec as P

HD = 128


def from_root(block, axis, source):
    block = jnp.where(lax.axis_index(axis) == source, block, jnp.zeros_like(block))
    return lax.psum(block, axis)


def layer_norm(values, gain):
    values = values.astype(jnp.float32)
    center = values - jnp.mean(values, -1, keepdims=True)
    spread = jnp.mean(center * center, -1, keepdims=True)
    return center * lax.rsqrt(spread + 1e-05) * gain


def fetch_prefixes(prefix_store, prefix_owner):
    caches = []
    for group in range(prefix_owner.shape[0]):
        caches.append(from_root(prefix_store[0], "req", prefix_owner[group]))
    return jnp.stack(caches)


def project_rows(suffix, gain, w_qkv):
    gathered = lax.all_gather(suffix, "tp", axis=0, tiled=True)
    normed = layer_norm(gathered, gain).astype(jnp.bfloat16)
    projected = jnp.einsum(
        "srd,dce->srce", normed, w_qkv, preferred_element_type=jnp.float32
    ).astype(jnp.bfloat16)
    return (projected, gathered)


def attend(projected, cached, lengths):
    slot_count, slots_dev, _, local_width = projected.shape
    heads = local_width // HD
    prefix_rows = cached.shape[1]
    scale = HD ** (-0.5)
    queries = projected[:, :, 0].reshape(slot_count, slots_dev, heads, HD)
    keys_own = projected[:, :, 1].reshape(slot_count, slots_dev, heads, HD)
    values_own = projected[:, :, 2].reshape(slot_count, slots_dev, heads, HD)
    keys_pre = cached[:, :, 0].reshape(slots_dev, prefix_rows, heads, HD)
    values_pre = cached[:, :, 1].reshape(slots_dev, prefix_rows, heads, HD)
    scores_pre = (
        jnp.einsum("srhd,rphd->rhsp", queries, keys_pre, preferred_element_type=jnp.float32) * scale
    )
    scores_own = (
        jnp.einsum("srhd,trhd->rhst", queries, keys_own, preferred_element_type=jnp.float32) * scale
    )
    places = jnp.arange(slot_count, dtype=jnp.int32)
    visible = (places[None, None, None, :] <= places[None, None, :, None]) & (
        places[None, None, None, :] < lengths[:, None, None, None]
    )
    scores_own = jnp.where(visible, scores_own, -jnp.inf)
    highest = jnp.maximum(
        jnp.max(scores_pre, -1, keepdims=True), jnp.max(scores_own, -1, keepdims=True)
    )
    raised_pre = jnp.exp(scores_pre - highest)
    raised_own = jnp.exp(scores_own - highest)
    total = jnp.sum(raised_pre, -1, keepdims=True) + jnp.sum(raised_own, -1, keepdims=True)
    weights_pre = (raised_pre / total).astype(jnp.bfloat16)
    weights_own = (raised_own / total).astype(jnp.bfloat16)
    context = jnp.einsum(
        "rhsp,rphd->srhd", weights_pre, values_pre, preferred_element_type=jnp.float32
    )
    context = context + jnp.einsum(
        "rhst,trhd->srhd", weights_own, values_own, preferred_element_type=jnp.float32
    )
    return context.reshape(slot_count, slots_dev, local_width).astype(jnp.bfloat16)


def on_device(
    suffix,
    prefix_store,
    prefix_owner,
    prefix_group,
    request_perm,
    suffix_len,
    ln_gain_attn,
    w_qkv,
    w_out_attn,
    ln_gain_mlp,
    w_in,
    w_down,
):
    part_rows, slots_dev, _ = suffix.shape
    slots = lax.axis_index("req") * slots_dev + jnp.arange(slots_dev, dtype=jnp.int32)
    requests = jnp.take(request_perm, slots)
    lengths = jnp.take(suffix_len, requests)
    groups = jnp.take(prefix_group, requests)
    stacked = fetch_prefixes(prefix_store, prefix_owner)
    projected, gathered = project_rows(suffix, ln_gain_attn, w_qkv)
    cached = jnp.take(stacked, groups, axis=0)
    context = attend(projected, cached, lengths)
    first_row = lax.axis_index("tp") * part_rows
    block = context
    attention = lax.psum_scatter(
        jnp.einsum("srk,kd->srd", block, w_out_attn, preferred_element_type=jnp.float32).astype(
            jnp.bfloat16
        ),
        "tp",
        scatter_dimension=0,
        tiled=True,
    ).astype(jnp.float32)
    hidden = (suffix.astype(jnp.float32) + attention).astype(jnp.bfloat16)
    normed = layer_norm(hidden, ln_gain_mlp).astype(jnp.bfloat16)
    product = jnp.einsum(
        "srd,df->srf",
        lax.all_gather(normed, "tp", axis=0, tiled=True),
        w_in,
        preferred_element_type=jnp.float32,
    )
    inner = jax.nn.gelu(product, approximate=False).astype(jnp.bfloat16)
    block = inner
    down = lax.psum_scatter(
        jnp.einsum("srf,fd->srd", block, w_down, preferred_element_type=jnp.float32).astype(
            jnp.bfloat16
        ),
        "tp",
        scatter_dimension=0,
        tiled=True,
    ).astype(jnp.float32)
    places = first_row + jnp.arange(part_rows, dtype=jnp.int32)
    valid = places[:, None] < lengths[None, :]
    return jnp.where(valid[:, :, None], hidden.astype(jnp.float32) + down, 0.0).astype(jnp.bfloat16)


def solution(mesh):
    placed = (
        P("tp", "req", None),
        P("req", None, None, "tp"),
        P(),
        P(),
        P(),
        P(),
        P(),
        P(None, None, "tp"),
        P("tp", None),
        P(),
        P(None, "tp"),
        P("tp", None),
    )
    return jax.shard_map(
        on_device, mesh=mesh, in_specs=placed, out_specs=P("tp", "req", None), check_vma=False
    )
```

profile of v0, /device:TPU:1, one launch (start us, length us, event | category | flops | bytes accessed | tf_op | source)
XLA Modules:
  0.0 555.5 jit_solution(3519037379020641564)
XLA Ops:
  7.4 0.7 all-gather.3.cloned.1.call-update
  8.1 0.0 all-reduce.3.cloned.1.call-start
  8.1 1.4 fusion.112
  10.8 4.0 broadcast_select_fusion
  14.8 0.0 reduce-scatter.3.cloned.1.call-start
  14.9 0.5 copy-done.2
  15.5 0.6 gather_fusion.2
  16.1 0.6 gather_fusion.4
  16.8 0.6 gather_fusion.3
  17.5 0.1 iota_compare_fusion.1
  17.6 0.1 broadcast_and_fusion
  17.7 54.1 %all-gather.3.cloned.1.call-done = bf16[256,2,2048]{2,1,0:T(2,128)(2,1)} async-done(((bf16[32,2,2048]{2,1,0:T(2,128)(2,1)}), bf16[256,2,2048]{2,1,0:T(2,128)(2,1)}) %all-gather.3.cloned.1.call-update) | async-done | bytes 2097168 | tf_op jit(solution)/shard_map/all_gather | solution.py:29
  71.8 3.4 convert_reduce_fusion
  75.3 2.9 fusion.3
  78.2 3.3 fusion.12
  81.5 1.9 fusion.14
  83.4 0.8 fusion.111
  84.2 0.4 fusion.113
  84.5 254.9 %all-reduce.3.cloned.1.call-done = (bf16[1,2048,2,256]{3,1,2,0:T(8,128)(2,1)}, bf16[1,2048,2,256]{3,1,2,0:T(8,128)(2,1)}) async-done(((bf16[1,2048,2,256]{3,1,2,0:T(8,128)(2,1)}, bf16[1,2048,2,256]{3,1,2,0:T(8,128)(2,1)}), (bf16[1,2048,2,256]{3,1,2,0:T(8,128)(2,1)}, bf16[1,2048,2,256]{3,1,2,0:T(8,128)(2,1)})) %all-reduce.3.cloned.1.call-update) | async-done | bytes 4194320 | tf_op jit(solution)/shard_map/psum | solution.py:11
  339.5 1.9 constant_dynamic-update-slice_fusion.1
  341.3 0.3 copy-done.6
  341.7 0.1 constant_dynamic-update-slice_fusion
  341.8 2.2 fusion.110
  344.0 2.3 gather_fusion.1
  346.3 3.6 gather_fusion
  349.9 2.8 maximum_select_fusion
  352.7 1.6 fusion.109
  354.3 2.5 copy.50
  356.8 2.9 copy.53
  359.8 1.4 multiply_reduce_fusion
  361.2 1.6 fusion
  362.8 0.2 fusion.31
  363.0 2.8 fusion.6
  365.9 0.3 fusion.29
  366.2 0.9 copy-done.8
  367.1 2.1 convolution_convert_fusion
  369.2 0.0 all-gather.5.cloned.1.call-start
  369.2 54.1 %reduce-scatter.3.cloned.1.call-done = bf16[32,2,2048]{2,0,1:T(8,128)(2,1)} async-done(((bf16[256,2,2048]{2,0,1:T(8,128)(2,1)}), bf16[32,2,2048]{2,0,1:T(8,128)(2,1)}) %reduce-scatter.3.cloned.1.call-update) | async-done | bytes 262160 | tf_op jit(solution)/shard_map/reduce_scatter | solution.py:100
  423.4 1.1 convert_reduce_fusion.1
  424.5 0.2 fusion.66
  424.7 0.9 fusion.68
  425.7 54.0 %all-gather.5.cloned.1.call-done = bf16[256,2,2048]{2,0,1:T(8,128)(2,1)} async-done(((bf16[32,2,2048]{2,0,1:T(8,128)(2,1)}), bf16[256,2,2048]{2,0,1:T(8,128)(2,1)}) %all-gather.5.cloned.1.call-update) | async-done | bytes 2097168 | tf_op jit(solution)/shard_map/all_gather | solution.py:112
  479.7 4.4 fusion.74
  484.1 7.7 %convolution_convert_fusion.1 = bf16[256,2,2048]{2,0,1:T(8,128)(2,1)} fusion(bf16[640,2048]{1,0:T(8,128)(2,1)} %param.25, f32[256,2,640]{2,0,1:T(8,128)S(1)} %get-tuple-element.29, u8[256,640]{1,0:T(8,128)(4,1)S(1)} %get-tuple-element.7, u8[256,640]{1,0:T(8,128)(4,1)S(1)} %get-tuple-element.6), kind=kOutput, calls=%fused_computation.21 | convolution fusion | flops 1366163456 | bytes 6356992 | tf_op jit(solution)/shard_map/srf,fd->srd/dot_general | solution.py:119
  491.9 0.1 broadcast_compare_fusion
  492.0 54.4 %reduce-scatter.5.cloned.1.call-done = bf16[32,2,2048]{2,0,1:T(8,128)(2,1)} async-done(((bf16[256,2,2048]{2,0,1:T(8,128)(2,1)}), bf16[32,2,2048]{2,0,1:T(8,128)(2,1)}) %reduce-scatter.5.cloned.1.call-update) | async-done | bytes 262160 | tf_op jit(solution)/shard_map/reduce_scatter | solution.py:118
  546.3 1.0 fusion.70
  547.4 1.0 copy.60
  (44 shorter events, 0.3 us)
Async XLA Ops:
  7.4 74.2 %copy-start = (bf16[2048,3,256]{2,0,1:T(8,128)(2,1)S(1)}, bf16[2048,3,256]{2,0,1:T(8,128)(2,1)}, u32[]{:S(2)}) copy-start(bf16[2048,3,256]{2,0,1:T(8,128)(2,1)} %param.21) | copy-start | bytes 9437188
  7.4 64.5 %all-gather.3.cloned.1.call-start = ((), (), s32[]{:S(2)}) async-start(), calls=%async_computation.2 | async-start | bytes 2359296 | tf_op jit(solution)/shard_map/all_gather | solution.py:29
  8.1 331.4 %all-reduce.3.cloned.1.call-start = ((), (), s32[]{:S(2)}) async-start(), calls=%async_computation.6 | async-start | bytes 8388608 | tf_op jit(solution)/shard_map/psum | solution.py:11
  14.8 0.7 copy-start.2
  14.8 1.3 copy-start.3
  14.8 2.0 copy-start.4
  14.8 408.5 %reduce-scatter.3.cloned.1.call-start = ((), (), s32[]{:S(2)}) async-start(), calls=%async_computation.3 | async-start | bytes 2359296 | tf_op jit(solution)/shard_map/reduce_scatter | solution.py:100
  17.7 60.5 %copy-start.11 = (f32[2048]{0:T(1024)S(1)}, f32[2048]{0:T(1024)}, u32[]{:S(2)}) copy-start(f32[2048]{0:T(1024)} %param.20) | copy-start | bytes 24580
  71.8 3.5 copy-start.5
  339.5 2.2 copy-start.6
  361.2 1.8 copy-start.7
  363.0 2.8 copy-start.10
  365.9 1.2 copy-start.8
  367.1 56.3 %copy-start.9 = (bf16[32,2,2048]{2,1,0:T(2,128)(2,1)S(1)}, bf16[32,2,2048]{2,1,0:T(2,128)(2,1)}, u32[]{:S(2)}) copy-start(bf16[32,2,2048]{2,1,0:T(2,128)(2,1)} %param.14) | copy-start | bytes 786436
  369.2 55.6 %copy-start.12 = (f32[2048]{0:T(1024)S(1)}, f32[2048]{0:T(1024)}, u32[]{:S(2)}) copy-start(f32[2048]{0:T(1024)} %param.23) | copy-start | bytes 24580
  369.2 110.5 %all-gather.5.cloned.1.call-start = ((), (), s32[]{:S(2)}) async-start(), calls=%async_computation.4 | async-start | bytes 2359296 | tf_op jit(solution)/shard_map/all_gather | solution.py:112
  425.6 120.7 %reduce-scatter.5.cloned.1.call-start = ((), (), s32[]{:S(2)}) async-start(), calls=%async_computation.5 | async-start | bytes 2359296 | tf_op jit(solution)/shard_map/reduce_scatter | solution.py:118
  484.1 64.3 %copy-start.1 = (bf16[2048,3,256]{2,0,1:T(8,128)(2,1)S(1)}, bf16[2048,3,256]{2,0,1:T(8,128)(2,1)}, u32[]{:S(2)}) copy-start(bf16[2048,3,256]{2,0,1:T(8,128)(2,1)} %param.21) | copy-start | bytes 9437188
Sparse Core Ops, SparseCore 0:
  10.0 61.8 all-gather.2
  369.3 53.9 reduce-scatter.2
  425.7 53.9 all-gather.4
  492.0 54.2 reduce-scatter.4
Sparse Core Ops, SparseCore 1:
  14.9 324.5 all-reduce.2
where the time goes:
time: 556 us; the launch traced here: 555 us
  waiting for transfers between devices  472 us (85%)
  local copies, waits for them, and re-layouts  23.9 us (4%)
  other arithmetic  21.9 us (4%)
  matrix products  21 us (4%)
  between operations  16.1 us (3%)
    psum x1, waiting for transfers between devices, from_root(): return lax.psum(block, axis)  255 us
    reduce_scatter x1, waiting for transfers between devices, on_device(): lax.psum_scatter(jnp.einsum('srf,fd->srd', block, w_down, preferred_eleme...  54.4 us
    reduce_scatter x1, waiting for transfers between devices, on_device(): lax.psum_scatter(jnp.einsum('srk,kd->srd', block, w_out_attn, preferred_e...  54.1 us
    all_gather x1, waiting for transfers between devices, project_rows(): gathered = lax.all_gather(suffix, 'tp', axis=0, tiled=True)  54.1 us
    all_gather x1, waiting for transfers between devices, on_device(): lax.all_gather(normed, 'tp', axis=0, tiled=True)  54 us
  transfers between devices with their start and end apart: 5, of which 5 were waited for; matrix products, arithmetic and copies ran while one was open for 4% of the time, Pallas kernels for 0%

commit v1 on v0

--- a/solution.py
+++ b/solution.py
@@ -109,7 +109,9 @@
     normed = layer_norm(hidden, ln_gain_mlp).astype(jnp.bfloat16)
     product = jnp.einsum(
         "srd,df->srf",
-        lax.all_gather(normed, "tp", axis=0, tiled=True),
+        jnp.concatenate(
+            lax.all_to_all(jnp.stack([normed] * lax.axis_size("tp")), "tp", 0, 0), axis=0
+        ),
         w_in,
         preferred_element_type=jnp.float32,
     )

time: 556 us -> 529 us (0.951)
  waiting for transfers between devices: 472 us -> 420 us
  blocking collectives: 0 us -> 29.2 us
    all_gather x1 -> x0, waiting for transfers between devices: 54 us -> none  [on_device(): lax.all_gather(normed, 'tp', axis=0, tiled=True)]
    all_to_all x0 -> x1, blocking collectives: none -> 29.2 us  [on_device(): lax.all_to_all(jnp.stack([normed] * lax.axis_size('tp')), 'tp', 0, 0)]
  transfers between devices with their start and end apart: 5 -> 4, of which waited for: 5 -> 4; matrix products, arithmetic and copies ran while one was open for 4% -> 4% of each run, Pallas kernels for 0% -> 0%
where the time goes in v1:
time: 529 us
  waiting for transfers between devices  420 us (79%)
  blocking collectives  29.2 us (6%)
  local copies, waits for them, and re-layouts  26 us (5%)
  other arithmetic  21.3 us (4%)
  matrix products  16.5 us (3%)
  between operations  16.1 us (3%)
    psum x1, waiting for transfers between devices, from_root(): return lax.psum(block, axis)  255 us
    reduce_scatter x1, waiting for transfers between devices, on_device(): lax.psum_scatter(jnp.einsum('srf,fd->srd', block, w_down, preferred_eleme...  55.5 us
    reduce_scatter x1, waiting for transfers between devices, on_device(): lax.psum_scatter(jnp.einsum('srk,kd->srd', block, w_out_attn, preferred_e...  54.4 us
    all_gather x1, waiting for transfers between devices, project_rows(): gathered = lax.all_gather(suffix, 'tp', axis=0, tiled=True)  54.1 us
    all_to_all x1, blocking collectives, on_device(): lax.all_to_all(jnp.stack([normed] * lax.axis_size('tp')), 'tp', 0, 0)  29.2 us
  transfers between devices with their start and end apart: 4, of which 4 were waited for; matrix products, arithmetic and copies ran while one was open for 4% of the time, Pallas kernels for 0%

profile of v1, /device:TPU:1, one launch (start us, length us, event | category | flops | bytes accessed | tf_op | source)
XLA Modules:
  0.0 528.8 jit_solution(14196647458555126264)
XLA Ops:
  7.4 0.7 all-gather.2.cloned.1.call-update
  8.1 1.4 fusion.112
  10.8 4.0 broadcast_select_fusion
  14.9 0.5 copy-done.2
  15.5 0.6 gather_fusion.2
  16.1 0.6 gather_fusion.4
  16.8 0.6 gather_fusion.3
  17.5 0.1 iota_compare_fusion.1
  17.6 0.1 broadcast_and_fusion
  17.7 54.1 %all-gather.2.cloned.1.call-done = bf16[256,2,2048]{2,1,0:T(2,128)(2,1)} async-done(((bf16[32,2,2048]{2,1,0:T(2,128)(2,1)}), bf16[256,2,2048]{2,1,0:T(2,128)(2,1)}) %all-gather.2.cloned.1.call-update) | async-done | bytes 2097168 | tf_op jit(solution)/shard_map/all_gather | solution.py:29
  71.8 3.4 convert_reduce_fusion
  75.3 2.9 fusion.3
  78.2 3.3 fusion.12
  81.5 1.9 fusion.14
  83.4 0.8 fusion.111
  84.2 0.4 fusion.113
  84.5 254.8 %all-reduce.3.cloned.1.call-done = (bf16[1,2048,2,256]{3,1,2,0:T(8,128)(2,1)}, bf16[1,2048,2,256]{3,1,2,0:T(8,128)(2,1)}) async-done(((bf16[1,2048,2,256]{3,1,2,0:T(8,128)(2,1)}, bf16[1,2048,2,256]{3,1,2,0:T(8,128)(2,1)}), (bf16[1,2048,2,256]{3,1,2,0:T(8,128)(2,1)}, bf16[1,2048,2,256]{3,1,2,0:T(8,128)(2,1)})) %all-reduce.3.cloned.1.call-update) | async-done | bytes 4194320 | tf_op jit(solution)/shard_map/psum | solution.py:11
  339.3 1.9 constant_dynamic-update-slice_fusion.1
  341.2 0.3 copy-done.6
  341.5 0.1 constant_dynamic-update-slice_fusion
  341.7 2.2 fusion.110
  343.9 2.3 gather_fusion.1
  346.2 3.6 gather_fusion
  349.7 2.8 maximum_select_fusion
  352.6 1.6 fusion.109
  354.2 2.5 copy.50
  356.7 2.9 copy.53
  359.6 1.4 multiply_reduce_fusion
  361.0 1.6 fusion
  362.7 0.2 fusion.31
  362.9 2.8 fusion.6
  365.7 0.3 fusion.29
  366.1 0.9 copy-done.8
  366.9 2.1 convolution_convert_fusion
  369.1 54.4 %reduce-scatter.3.cloned.1.call-done = bf16[32,2,2048]{2,0,1:T(8,128)(2,1)} async-done(((bf16[256,2,2048]{2,0,1:T(8,128)(2,1)}), bf16[32,2,2048]{2,0,1:T(8,128)(2,1)}) %reduce-scatter.3.cloned.1.call-update) | async-done | bytes 262160 | tf_op jit(solution)/shard_map/reduce_scatter | solution.py:100
  423.5 1.1 convert_reduce_fusion.1
  424.6 0.2 fusion.66
  424.8 0.2 fusion.68
  425.0 0.2 stack.11
  425.3 29.2 %all_to_all.5 = bf16[8,32,2,2048]{3,1,2,0:T(8,128)(2,1)S(1)} all-to-all(bf16[8,32,2,2048]{3,1,2,0:T(8,128)(2,1)S(1)} %stack.11), channel_id=1, replica_groups=mesh['req'=32,'tp'=8] {'tp'}, dimensions={0} | all-to-all | bytes 4194304 | tf_op jit(solution)/shard_map/all_to_all | solution.py:113
  454.5 0.1 copy.60
  454.7 1.6 copy-done.13
  456.3 2.0 fusion.74
  458.3 5.7 %convolution_convert_fusion.1 = bf16[256,2,2048]{2,0,1:T(8,128)(2,1)} fusion(bf16[640,2048]{1,0:T(8,128)(2,1)S(1)} %copy-done.14, f32[256,2,640]{2,0,1:T(8,128)S(1)} %get-tuple-element.29, u8[256,640]{1,0:T(8,128)(4,1)S(1)} %get-tuple-element.7, u8[256,640]{1,0:T(8,128)(4,1)S(1)} %get-tuple-element.6), kind=kOutput, calls=%fused_computation.21 | convolution fusion | flops 1366163456 | bytes 6356992 | tf_op jit(solution)/shard_map/srf,fd->srd/dot_general | solution.py:121
  464.0 0.1 broadcast_compare_fusion
  464.1 55.5 %reduce-scatter.5.cloned.1.call-done = bf16[32,2,2048]{2,0,1:T(8,128)(2,1)} async-done(((bf16[256,2,2048]{2,0,1:T(8,128)(2,1)}), bf16[32,2,2048]{2,0,1:T(8,128)(2,1)}) %reduce-scatter.5.cloned.1.call-update) | async-done | bytes 262160 | tf_op jit(solution)/shard_map/reduce_scatter | solution.py:120
  519.6 1.0 fusion.70
  520.7 1.0 copy.61
  (48 shorter events, 0.4 us)
Async XLA Ops:
  7.4 74.2 %copy-start = (bf16[2048,3,256]{2,0,1:T(8,128)(2,1)S(1)}, bf16[2048,3,256]{2,0,1:T(8,128)(2,1)}, u32[]{:S(2)}) copy-start(bf16[2048,3,256]{2,0,1:T(8,128)(2,1)} %param.21) | copy-start | bytes 9437188
  7.4 64.5 %all-gather.2.cloned.1.call-start = ((), (), s32[]{:S(2)}) async-start(), calls=%async_computation.3 | async-start | bytes 2359296 | tf_op jit(solution)/shard_map/all_gather | solution.py:29
  8.1 331.2 %all-reduce.3.cloned.1.call-start = ((), (), s32[]{:S(2)}) async-start(), calls=%async_computation.6 | async-start | bytes 8388608 | tf_op jit(solution)/shard_map/psum | solution.py:11
  14.8 0.7 copy-start.2
  14.8 1.3 copy-start.3
  14.8 2.0 copy-start.4
  14.8 408.6 %reduce-scatter.3.cloned.1.call-start = ((), (), s32[]{:S(2)}) async-start(), calls=%async_computation.4 | async-start | bytes 2359296 | tf_op jit(solution)/shard_map/reduce_scatter | solution.py:100
  17.7 60.5 %copy-start.11 = (f32[2048]{0:T(1024)S(1)}, f32[2048]{0:T(1024)}, u32[]{:S(2)}) copy-start(f32[2048]{0:T(1024)} %param.20) | copy-start | bytes 24580
  71.8 3.5 copy-start.5
  339.3 2.2 copy-start.6
  361.0 1.8 copy-start.7
  362.9 2.8 copy-start.10
  365.7 1.2 copy-start.8
  366.9 56.5 %copy-start.9 = (bf16[32,2,2048]{2,1,0:T(2,128)(2,1)S(1)}, bf16[32,2,2048]{2,1,0:T(2,128)(2,1)}, u32[]{:S(2)}) copy-start(bf16[32,2,2048]{2,1,0:T(2,128)(2,1)} %param.14) | copy-start | bytes 786436
  369.0 55.8 %copy-start.12 = (f32[2048]{0:T(1024)S(1)}, f32[2048]{0:T(1024)}, u32[]{:S(2)}) copy-start(f32[2048]{0:T(1024)} %param.23) | copy-start | bytes 24580
  369.1 150.6 %reduce-scatter.5.cloned.1.call-start = ((), (), s32[]{:S(2)}) async-start(), calls=%async_computation.5 | async-start | bytes 2359296 | tf_op jit(solution)/shard_map/reduce_scatter | solution.py:120
  454.5 1.7 copy-start.13
  456.3 2.0 copy-start.14
  458.3 63.3 %copy-start.1 = (bf16[2048,3,256]{2,0,1:T(8,128)(2,1)S(1)}, bf16[2048,3,256]{2,0,1:T(8,128)(2,1)}, u32[]{:S(2)}) copy-start(bf16[2048,3,256]{2,0,1:T(8,128)(2,1)} %param.21) | copy-start | bytes 9437188
Sparse Core Ops, SparseCore 0:
  10.0 61.8 all-gather.1
  369.2 54.2 reduce-scatter.2
  464.1 55.4 reduce-scatter.4
Sparse Core Ops, SparseCore 1:
  14.9 324.3 all-reduce.2
